TPU v7x, 512 devices: a whole 4x8x8 slice. The times are simulated.
512 devices in a mesh: seq: 64 (over y, z_lo, core), tp: 8 (over z_hi, x).
Axes of the slice: x: 4, y: 8, z: 8 (z_hi: 2, z_lo: 4; z = z_hi * 4 + z_lo), core: 2. Of those that a mesh axis runs over, the one named last changes fastest.
Arguments:
- stream: bfloat16 [8192, 8192], P('seq', 'tp'), may hold values from -6 to 6
- hidden: bfloat16 [14336, 8192], P('seq'), may hold values from -6 to 6
- final_gain: bfloat16 [8192], P('tp'), may hold values from 0.099609375 to 1.8984375
- value_head: bfloat16 [8192], P('tp'), may hold values from -0.0625 to 0.0625
- rewards: float32 [8192], P('seq'), may hold values from -3 to 3
- kl_terms: float32 [8192], P('seq'), may hold values from -6 to 6
- resets: int32 [8192], P('seq'), may hold values 0 or 1
Outputs:
- values: float32 [8192], P('seq')
- returns: float32 [8192], P('seq')
- grad_head: float32 [8192], P('tp')
- grad_down: bfloat16 [14336, 8192], P('seq', 'tp')
All inputs are finite; a program needn't handle non-finite values. No bound on the sum of `resets` on one device may be relied on, other than what follows from the above.
Results may differ from a plain program's by a relative error of at most 0.0049.
Values may be sent and summed in bfloat16 or wider, within the bound.
A program may use at most 64 MiB of HBM per device.

v0:
```python
import jax
import jax.numpy as jnp
from jax import lax
from jax.sharding import PartitionSpec as P

D = 8192


epsilon = 1e-05


def prefix(value, axis, join, neutral):
    count, mine = (lax.axis_size(axis), lax.axis_index(axis))
    pieces = jax.tree.map(lambda part: lax.all_gather(part, axis), value)
    pieces = jax.tree.map(lambda part: part[::-1], pieces)
    mine = count - 1 - mine
    total = jax.tree.map(
        lambda part, zero: jnp.full_like(part, 0) + jnp.asarray(zero, part.dtype), value, neutral
    )

    def step(position, total):
        longer = join(total, jax.tree.map(lambda part: part[position], pieces))
        return jax.tree.map(lambda new, old: jnp.where(position < mine, new, old), longer, total)

    return lax.fori_loop(0, count - 1, step, total)


def combine_carry(earlier, later):
    return (later[0] + later[1] * earlier[0], later[1] * earlier[1])


def body(stream, hidden, final_gain, value_head, rewards, kl_terms, resets):
    tok_local = stream.shape[0]
    stream_f = stream.astype(jnp.float32)
    head_vector = final_gain.astype(jnp.float32) * value_head.astype(jnp.float32)
    sum_squares, head_dot = lax.psum(
        (jnp.sum(stream_f * stream_f, axis=-1), jnp.sum(stream_f * head_vector, axis=-1)), "tp"
    )
    inv_rms = lax.rsqrt(sum_squares / D + epsilon)
    values = inv_rms * head_dot
    step_reward = rewards - 0.2 * kl_terms
    before = jnp.cumsum(resets) - resets
    total_resets = jnp.sum(resets)
    positions = jnp.arange(tok_local)
    reach_mask = (positions[None, :] >= positions[:, None]) & (before[None, :] == before[:, None])
    local_return = jnp.sum(jnp.where(reach_mask, step_reward[None, :], 0.0), axis=1)
    passing = jnp.where(before == total_resets, 1.0, 0.0).astype(jnp.float32)
    shard_value = local_return[0]
    shard_pass = passing[0]
    incoming, _ = prefix(
        (shard_value, shard_pass),
        "seq",
        combine_carry,
        (jnp.zeros((), jnp.float32), jnp.ones((), jnp.float32)),
    )
    returns = local_return + passing * incoming
    value_error = values - returns
    head_total = lax.psum(jnp.sum((value_error * inv_rms)[:, None] * stream_f, axis=0), "seq")
    grad_head = final_gain.astype(jnp.float32) * head_total
    dstream = (
        value_error[:, None]
        * (inv_rms[:, None] * head_vector - (inv_rms**3 * head_dot / D)[:, None] * stream_f)
    ).astype(jnp.bfloat16)
    grad_sum = jnp.dot(
        hidden,
        lax.all_gather(dstream, "seq", axis=0, tiled=True),
        preferred_element_type=jnp.float32,
    )
    grad_down = grad_sum.astype(jnp.bfloat16)
    return (values, returns, grad_head, grad_down)


def solution(mesh):
    placed = (P("seq", "tp"), P("seq", None), P("tp"), P("tp"), P("seq"), P("seq"), P("seq"))
    return jax.shard_map(
        body,
        mesh=mesh,
        in_specs=placed,
        out_specs=(P("seq"), P("seq"), P("tp"), P("seq", "tp")),
        check_vma=False,
    )
```

profile of v0, /device:TPU:1, one launch (start us, length us, event | category | flops | bytes accessed | tf_op | source)
XLA Modules:
  0.0 514.1 jit_solution(15641219484688983226)
XLA Ops:
  7.2 1.3 reduce_sum.48
  8.5 0.8 copy.13
  9.5 1.3 dynamic-slice
  10.8 1.3 compare_select_fusion
  12.3 0.7 slice_dynamic-update-slice_fusion
  13.1 0.7 slice_dynamic-update-slice_fusion.1
  13.8 139.6 %all-reduce.2 = (f32[64]{0:T(128)S(1)}, f32[64]{0:T(128)S(1)}) all-reduce(f32[64]{0:T(128)S(1)} %slice_dynamic-update-slice_fusion.1, f32[64]{0:T(128)S(1)} %slice_dynamic-update-slice_fusion), channel_id=1, replica_groups=mesh['seq'=64,'tp'=8] {'seq'}, use_global_device_ids=true, to_apply=%add | all-reduce | flops 128 | bytes 1024
  153.7 164.9 %while.13 = (s32[]{:T(128)}, f32[]{:T(128)}, s32[]{:T(128)}, f32[64]{0:T(128)S(1)}, f32[64]{0:T(128)S(1)}, /*index=5*/s32[]{:T(128)}) while((s32[]{:T(128)}, f32[]{:T(128)}, s32[]{:T(128)}, f32[64]{0:T(128)S(1)}, f32[64]{0:T(128)S(1)}, /*index=5*/s32[]{:T(128)}) %tuple.41), condition=%wide.region_8.9_spmd, body=%wide.region_7.8_spmd.sunk | while | flops 6 | bytes 147 | solution.py:25
  154.2 0.7 dynamic_slice.17
  156.9 0.7 dynamic_slice.17
  159.5 0.7 dynamic_slice.17
  162.1 0.7 dynamic_slice.17
  164.7 0.7 dynamic_slice.17
  167.3 0.7 dynamic_slice.17
  170.0 0.7 dynamic_slice.17
  172.6 0.7 dynamic_slice.17
  175.2 0.7 dynamic_slice.17
  177.8 0.7 dynamic_slice.17
  180.4 0.7 dynamic_slice.17
  183.0 0.7 dynamic_slice.17
  185.7 0.7 dynamic_slice.17
  188.3 0.7 dynamic_slice.17
  190.9 0.7 dynamic_slice.17
  193.5 0.7 dynamic_slice.17
  196.1 0.7 dynamic_slice.17
  198.8 0.7 dynamic_slice.17
  201.4 0.7 dynamic_slice.17
  204.0 0.7 dynamic_slice.17
  206.6 0.7 dynamic_slice.17
  209.2 0.7 dynamic_slice.17
  211.9 0.7 dynamic_slice.17
  232.8 0.7 dynamic_slice.17
  235.4 0.7 dynamic_slice.17
  238.0 0.7 dynamic_slice.17
  240.7 0.7 dynamic_slice.17
  243.3 0.7 dynamic_slice.17
  282.5 0.7 dynamic_slice.17
  285.2 0.7 dynamic_slice.17
  287.8 0.7 dynamic_slice.17
  290.4 0.7 dynamic_slice.17
  293.0 0.7 dynamic_slice.17
  318.6 0.7 convert_multiply_fusion.5
  319.3 1.1 fusion.1
  320.4 26.7 %all-reduce.3 = (f32[128]{0:T(128)S(1)}, f32[128]{0:T(128)S(1)}) all-reduce(f32[128]{0:T(128)S(1)} %get-tuple-element.100, f32[128]{0:T(128)S(1)} %get-tuple-element.99), channel_id=1, replica_groups=mesh['seq'=64,'tp'=8] {'tp'}, use_global_device_ids=true, to_apply=%region_3.0 | all-reduce | flops 256 | bytes 2048 | tf_op jit(solution)/shard_map/psum | solution.py:36
  347.7 1.9 fusion.6
  349.6 144.7 %psum.23 = f32[1024]{0:T(1024)S(1)} all-reduce(f32[1024]{0:T(1024)S(1)} %get-tuple-element.122), channel_id=1, replica_groups=mesh['seq'=64,'tp'=8] {'seq'}, use_global_device_ids=true, to_apply=%region_10.11 | all-reduce | flops 1024 | bytes 8192 | tf_op jit(solution)/shard_map/psum | solution.py:58
  494.4 1.3 convert_multiply_fusion.4
  495.7 11.6 %fusion = bf16[224,1024]{1,0:T(8,128)(2,1)} fusion(bf16[224,8192]{1,0:T(8,128)(2,1)} %param.10, bf16[8192,1024]{1,0:T(8,128)(2,1)} %all-gather.2.cloned.1.call-done), kind=kOutput, calls=%fused_computation.1 | convolution fusion | flops 3758325760 | bytes 20905984 | tf_op jit(solution)/shard_map/dot_general | solution.py:64
  (104 shorter events, 58.0 us)
Async XLA Ops:
  7.2 488.5 %all-gather.2.cloned.1.call-start = ((), (), s32[]{:S(2)}) async-start(), calls=%async_computation | async-start | bytes 17039360 | tf_op jit(solution)/shard_map/all_gather | solution.py:66
Sparse Core Ops, SparseCore 0:
  349.8 133.9 all-gather.1
where the time goes:
time: 516 us; the launch traced here: 514 us
  blocking collectives  311 us (60%)
  loops' own time  86.3 us (17%)
  local copies, waits for them, and re-layouts  82.4 us (16%)
  between operations  14.1 us (3%)
  matrix products  11.6 us (2%)
  other arithmetic  8.64 us (2%)
    psum x1, blocking collectives, body(): lax.psum(jnp.sum((value_error * inv_rms)[:, None] * stream_f, axis=0), 's...  145 us
    unnamed x1, blocking collectives  140 us
    another operation x1, loops' own time, prefix(): return lax.fori_loop(0, count - 1, step, total)  86.3 us
    dynamic_slice x126, local copies, waits for them, and re-layouts, step(): longer = join(total, jax.tree.map(lambda part: part[position], pieces))  78.6 us
    psum x1, blocking collectives, body(): lax.psum((jnp.sum(stream_f * stream_f, axis=-1), jnp.sum(stream_f * head_...  26.7 us
    dot_general x1, matrix products, body(): jnp.dot(hidden, lax.all_gather(dstream, 'seq', axis=0, tiled=True), prefe...  11.6 us
  transfers between devices with their start and end apart: 1, of which 0 were waited for; matrix products, arithmetic and copies ran while one was open for 0% of the time, Pallas kernels for 0%

commit v1 on v0

v1 whole, which is shorter than its diff:
```python
import functools

import jax
import jax.numpy as jnp
from jax import lax
from jax.experimental import pallas as pl
from jax.experimental.pallas import tpu as pltpu
from jax.sharding import PartitionSpec as P

MESH = pl.DeviceIdType.MESH
D = 8192
EPS = 1e-05
NY, NZ, NX, NT = 8, 4, 4, 8
TOK, COLS, ROWS = 128, 1024, 224
WIDTHS = (256, 256, 256, 256)
OFFS = tuple(sum(WIDTHS[:j]) for j in range(len(WIDTHS)))
C = len(WIDTHS)
START = 3.0
HOPS = ((4, 3), (3, 4))


def ring_plan(direction):
    unit, lag = [w * 0.0055 for w in WIDTHS], 2.0
    ready, order, arrival, now, z = {}, [], {}, 0.0, 0.0
    for j in range(C):
        z += unit[j]
        ready[(0, j, 1)] = 0.0
        ready[(1, j, 1)] = 3.0 + z
    while ready:
        able = [m for m in ready if ready[m] <= now + 1e-9]
        if not able:
            now = min(ready.values())
            continue
        m = min(able, key=lambda m: (m[1], m[2], m[0]))
        del ready[m]
        plane, j, hop = m
        order.append((now, m))
        now += unit[j]
        arrival[m] = now + lag
        if hop < HOPS[direction][plane]:
            ready[(plane, j, hop + 1)] = arrival[m]
    return order, arrival


def timeline():
    todo, arrivals = [], []
    for direction in (0, 1):
        order, arrival = ring_plan(direction)
        arrivals.append(arrival)
        for t, (plane, j, hop) in order:
            if (plane, hop) != (0, 1) or t > START:
                todo.append((t, 0, 0.05, ("ring", direction, plane, j, hop)))
    todo += [(7.0, 0, 0.05, ("share", 0)), (12.0, 0, 0.05, ("share", 1))]
    todo += [(17.0, 0, 0.05, ("pass", 0)), (21.0, 0, 0.05, ("pass", 1))]
    todo += [(7.0, 1, 0.3, ("first",)), (13.0, 1, 0.4, ("second",))]
    todo += [(21.0 + 0.1 * i, 2, 0.2, ("coef", i)) for i in range(NY)]
    todo += [(27.0, 0, 0.0, ("hidden",))]
    for j in range(C):
        for d in range(-3, 5):
            if d == 4:
                t = max(arrivals[0][(0, j, 4)], arrivals[1][(1, j, 4)])
            elif d == 0:
                t = 0.0
            else:
                side = 0 if d < 0 else 1
                t = max(arrivals[side][(plane, j, abs(d))] for plane in (0, 1))
            todo.append((max(27.1, t + 0.5), 3 + j, 0.4, ("piece", j, d)))
    now, order, left = 0.0, [], dict.fromkeys(range(C), NY)
    while todo:
        able = [e for e in todo if e[0] <= now + 1e-9]
        if not able:
            now = min(e[0] for e in todo)
            continue
        e = min(able, key=lambda e: (e[1], e[0]))
        todo.remove(e)
        order.append(e[3])
        now += e[2]
        if e[3][0] == "piece":
            j = e[3][1]
            left[j] -= 1
            if left[j] == 0:
                order.append(("reduce", j))
                todo.append((now + 2.5, 1, 0.2, ("swap", j)))
        if e[3][0] == "swap":
            todo.append((now + 6.0, 1, 0.2, ("write", e[3][1])))
    return order


def kernel(*refs):
    refs = list(refs)
    take = lambda n: [refs.pop(0) for _ in range(n)]
    stream, hidden, gain, head_in, rewards, kl_terms, resets = take(7)
    values_out, returns_out, head_out, down_out = take(4)
    (X,) = take(1)
    S, ACC, P1, T2, P2 = take(C), take(C), take(C), take(C), take(C)
    H, ST, PA, PB, CO, AC, BC, GP, GQ = take(9)
    ring_send, ring_recv, swap_send, swap_recv, down_send, down_recv, small_send, small_recv, hid_send, hid_recv, local = take(11)

    s, t = lax.axis_index("seq"), lax.axis_index("tp")
    y, z, c = s // 8, (s // 2) % 4, s % 2
    zb, zp, q = z % 2, z // 2, s % 8
    h, x = t // 4, t % 4
    oz, oc = z + 1 - 2 * zb, 1 - c
    fz = z + 2 - 4 * zp
    mine = zb * 2 + c

    def seq(y, z, c):
        return (y * 4 + z) * 2 + c

    def up(d):
        return lax.rem(y + 16 + d, NY)

    def remote(src, dst, send, recv, device):
        return pltpu.make_async_remote_copy(
            src_ref=src, dst_ref=dst, send_sem=send, recv_sem=recv, device_id=device, device_id_type=MESH
        )

    def drain(ref, sem):
        pltpu.make_async_copy(ref, ref, sem).wait()

    x_copy = pltpu.make_async_copy(stream, X, local.at[0])
    x_copy.start()
    own_copies = []
    for j in range(C):
        own_copies.append(
            pltpu.make_async_copy(stream.at[:, pl.ds(OFFS[j], WIDTHS[j])], S[j].at[y, zp], local.at[1 + j])
        )
        own_copies[-1].start()

    def tokens(yy, zz, cc):
        return pl.ds(pl.multiple_of(seq(yy, zz, cc) * TOK, TOK), TOK)

    def own_hidden(yy, _):
        for p in range(2):
            pltpu.make_async_copy(hidden.at[:, tokens(yy, zb + 2 * p, c)], H.at[mine, yy, p], local.at[1 + C]).start()
        return 0

    lax.fori_loop(0, NY, own_hidden, 0)

    line = []
    for d in range(1, 8):
        other = lax.rem(q + d, 8)
        line.append((y * 8 + other, t))
    column = [(seq(up(d), z, c), t) for d in range(1, NY)]
    far = [(seq(up(d), fz, c), t) for d in range(NY)]
    rank = [(s, lax.rem(t + d, NT)) for d in range(1, NT)]
    barrier = pltpu.get_barrier_semaphore()
    peers = line + column + far[1:] + rank
    for peer in peers:
        pl.semaphore_signal(barrier, inc=1, device_id=peer, device_id_type=MESH)

    row_id = lax.broadcasted_iota(jnp.int32, (TOK, TOK), 0)
    col_id = lax.broadcasted_iota(jnp.int32, (TOK, TOK), 1)

    def to_col(row):
        return jnp.sum(jnp.where(row_id == col_id, row, 0.0), axis=1, keepdims=True)

    def to_row(col):
        return jnp.sum(jnp.where(row_id == col_id, col, 0.0), axis=0, keepdims=True)

    head = gain[...].astype(jnp.float32) * head_in[...].astype(jnp.float32)
    res_row = resets[...].astype(jnp.float32)
    before_col = jnp.sum(jnp.where(col_id < row_id, res_row, 0.0), axis=1, keepdims=True)
    before_row = jnp.sum(jnp.where(row_id < col_id, to_col(res_row), 0.0), axis=0, keepdims=True)
    total = jnp.sum(res_row, axis=1, keepdims=True)
    reward_col = to_col(rewards[...] - 0.2 * kl_terms[...])
    reach = (row_id >= col_id) & (before_col == before_row)
    local_row = jnp.sum(jnp.where(reach, reward_col, 0.0), axis=0, keepdims=True)
    pass_row = jnp.where(before_row == total, 1.0, 0.0)

    def put(ref, index, first, second):
        ref[index] = jnp.zeros((8, TOK), jnp.float32)
        ref[index, 0:1, :] = jnp.broadcast_to(first, (1, TOK))
        ref[index, 1:2, :] = jnp.broadcast_to(second, (1, TOK))

    put(PA, q, local_row[:, 0:1], pass_row[:, 0:1])
    x_copy.wait()
    xf = X[...].astype(jnp.float32)
    put(
        ST,
        t,
        to_row(jnp.sum(xf * xf, axis=1, keepdims=True)),
        to_row(jnp.sum(xf * head, axis=1, keepdims=True)),
    )

    pl.semaphore_wait(barrier, len(peers))

    sends = []

    def go(copy):
        copy.start()
        sends.append(copy)

    def small(kind, n, ref, index, to):
        for i, peer in enumerate(to):
            go(remote(ref.at[index], ref.at[index], small_send.at[n + i], small_recv.at[kind], peer))

    def ring(direction, plane, j, hop):
        step = 1 if direction == 0 else -1
        slot = S[j].at[up(-step * (hop - 1)), zp if plane == 0 else 1 - zp]
        src = stream.at[:, pl.ds(OFFS[j], WIDTHS[j])] if (plane, hop) == (0, 1) else slot
        i = ((direction * 2 + plane) * C + j) * 4 + hop - 1
        return remote(src, slot, ring_send.at[i], ring_recv.at[i], (seq(up(step), z, c), t))

    def swap(j):
        return remote(
            stream.at[:, pl.ds(OFFS[j], WIDTHS[j])], S[j].at[y, zp], swap_send.at[j], swap_recv.at[j], (seq(y, fz, c), t)
        )

    first_sends = [{m[1]: at for at, m in ring_plan(d)[0] if m[0] == 0 and m[2] == 1} for d in (0, 1)]
    small(0, 0, ST, t, rank)
    small(1, 7, PA, q, line)
    for j in range(C):
        for direction in (0, 1):
            if first_sends[direction][j] <= START:
                go(ring(direction, 0, j, 1))
        go(swap(j))

    def pair_hidden(i, p, cc):
        yy = 2 * x + i
        return remote(
            hidden.at[:, tokens(yy, 1 - zb + 2 * p, cc)], H.at[mine, yy, p],
            hid_send.at[1 + i], hid_recv.at[1 + i], (seq(y, oz, cc), t),
        )

    for i in range(2):
        for p in range(2):
            for cc in range(2):
                pair_hidden(i, p, cc).start()

    def core_hidden(yy, _):
        for p in range(2):
            remote(
                hidden.at[:, tokens(yy, zb + 2 * p, oc)], H.at[mine, yy, p],
                hid_send.at[0], hid_recv.at[0], (seq(y, z, oc), t),
            ).start()
        return 0

    lax.fori_loop(0, NY, core_hidden, 0)

    def pair_block(yy):
        return H.at[pl.ds(2 * (1 - zb), 2), yy]

    def x_copy_to(direction, i, hop):
        step = 1 if direction == 0 else -1
        owner = lax.rem(x + 8 - step * (hop - 1), NX)
        block = pair_block(2 * owner + i)
        n = 3 + (hop - 1) * 4 + direction * 2 + i
        return remote(block, block, hid_send.at[n], hid_recv.at[n], (s, h * 4 + lax.rem(x + 4 + step, NX)))

    state = {}
    seen = set()

    def arrived(direction, plane, j, hop):
        if (direction, plane, j, hop) not in seen:
            seen.add((direction, plane, j, hop))
            step = 1 if direction == 0 else -1
            i = ((direction * 2 + plane) * C + j) * 4 + hop - 1
            drain(S[j].at[up(-step * hop), zp if plane == 0 else 1 - zp], ring_recv.at[i])

    def other_in(j):
        if ("swap", j) not in seen:
            seen.add(("swap", j))
            drain(S[j].at[y, 1 - zp], swap_recv.at[j])

    def do_ring(direction, plane, j, hop):
        if hop == 1 and plane == 1:
            other_in(j)
        elif hop > 1:
            arrived(direction, plane, j, hop - 1)
        go(ring(direction, plane, j, hop))

    def x_arrived(direction, i, hop):
        step = 1 if direction == 0 else -1
        owner = lax.rem(x + 8 - step * hop, NX)
        drain(pair_block(2 * owner + i), hid_recv.at[3 + (hop - 1) * 4 + direction * 2 + i])

    def do_share(i):
        drain(pair_block(2 * x + i), hid_recv.at[1 + i])
        for direction in (0, 1):
            go(x_copy_to(direction, i, 1))

    def do_pass(i):
        direction = i
        x_arrived(direction, i, 1)
        go(x_copy_to(direction, i, 2))

    def do_first():
        drain(ST.at[pl.ds(0, 7)], small_recv.at[0])
        drain(PA.at[pl.ds(0, 7)], small_recv.at[1])
        squares, along = jnp.zeros((1, TOK), jnp.float32), jnp.zeros((1, TOK), jnp.float32)
        for i in range(NT):
            squares += ST[i, 0:1, :]
            along += ST[i, 1:2, :]
        value, keep = jnp.zeros((1, TOK), jnp.float32), jnp.ones((1, TOK), jnp.float32)
        for i in reversed(range(8)):
            value = PA[i, 0:1, :] + PA[i, 1:2, :] * value
            keep = PA[i, 1:2, :] * keep
        put(PB, y, value, keep)
        small(2, 14, PB, y, column)
        mean = squares * (1.0 / D) + EPS
        scale = lax.rsqrt(mean)
        scale = scale * (1.5 - 0.5 * mean * scale * scale)
        values = scale * along
        values_out[...] = values
        state.update(scale=scale, along=along, values=values)

    def do_second():
        drain(PB.at[pl.ds(0, 7)], small_recv.at[2])
        carry = jnp.zeros((1, TOK), jnp.float32)
        my_y, my_q = jnp.full((1, TOK), y, jnp.int32), jnp.full((1, TOK), q, jnp.int32)
        for i in reversed(range(NY)):
            carry = jnp.where(my_y < i, PB[i, 0:1, :] + PB[i, 1:2, :] * carry, carry)
        for i in reversed(range(8)):
            carry = jnp.where(my_q < i, PA[i, 0:1, :] + PA[i, 1:2, :] * carry, carry)
        returns = local_row + pass_row * carry
        returns_out[...] = returns
        scale, along = state["scale"], state["along"]
        error = state["values"] - returns
        put(CO, y * 2 + zp, error * scale, error * (scale * scale * scale * along * (1.0 / D)))
        small(3, 21, CO, y * 2 + zp, column + far)

    def do_coef(i):
        if i == 0:
            drain(CO.at[pl.ds(0, 15)], small_recv.at[3])
        for p in range(2):
            block = slice(p * TOK, (p + 1) * TOK)
            AC[i, block, :] = jnp.broadcast_to(to_col(CO[i * 2 + p, 0:1, :]), (TOK, TOK))
            BC[i, block, :] = jnp.broadcast_to(to_col(CO[i * 2 + p, 1:2, :]), (TOK, TOK))

    def do_hidden():
        drain(H.at[mine], local.at[1 + C])
        drain(H.at[zb * 2 + oc], hid_recv.at[0])
        x_arrived(0, 1, 1)
        x_arrived(1, 0, 1)
        for direction in (0, 1):
            x_arrived(direction, direction, 2)

    def do_piece(j, d):
        w, off = WIDTHS[j], OFFS[j]
        if d == 0:
            own_copies[j].wait()
            other_in(j)
        elif d == 4:
            arrived(0, 0, j, 4)
            arrived(1, 1, j, 4)
        else:
            for plane in range(2):
                arrived(0 if d < 0 else 1, plane, j, abs(d))
        yy = up(d)
        a, b = AC[yy], BC[yy]
        xs = S[j][yy].reshape(2 * TOK, w)
        grads = []
        for i in range(w // TOK):
            xi = xs[:, i * TOK : (i + 1) * TOK].astype(jnp.float32)
            n = off // TOK + i
            GP[yy, n : n + 1, :] = jnp.sum(a * xi, axis=0, keepdims=True)
            grads.append((a * head[:, n * TOK : (n + 1) * TOK] - b * xi).astype(jnp.bfloat16))
        rows = [jnp.concatenate([H[r, yy, 0], H[r, yy, 1]], axis=1) for r in range(4)]
        out = jnp.dot(
            jnp.concatenate(rows, axis=0), jnp.concatenate(grads, axis=1), preferred_element_type=jnp.float32
        ).reshape(4, ROWS, w)
        if ("sum", j) not in seen:
            seen.add(("sum", j))
            ACC[j][...] = out
        else:
            ACC[j][...] += out

    def core_copy(j, k):
        return remote(
            ACC[j].at[k * 2 + oc], P1[j].at[k], down_send.at[j * 3 + k], down_recv.at[j * 3 + k], (seq(y, z, oc), t)
        )

    def pair_copy(j):
        return remote(T2[j], P2[j], down_send.at[j * 3 + 2], down_recv.at[j * 3 + 2], (seq(y, oz, c), t))

    def do_reduce(j):
        for k in range(2):
            go(core_copy(j, k))

    def do_swap(j):
        for k in range(2):
            core_copy(j, k).wait_recv()
        T2[j][...] = (ACC[j][(1 - zb) * 2 + c] + P1[j][1 - zb]).astype(jnp.bfloat16)
        go(pair_copy(j))

    def do_write(j):
        pair_copy(j).wait_recv()
        out = ACC[j][mine] + P1[j][zb] + P2[j][...].astype(jnp.float32)
        down_out[:, OFFS[j] : OFFS[j] + WIDTHS[j]] = out.astype(jnp.bfloat16)

    events = {
        "ring": do_ring, "share": do_share, "pass": do_pass, "first": do_first, "second": do_second,
        "coef": do_coef, "hidden": do_hidden, "piece": do_piece, "reduce": do_reduce, "swap": do_swap,
        "write": do_write,
    }
    order = timeline()
    last = max(i for i, e in enumerate(order) if e[0] == "piece")
    for i, e in enumerate(order):
        events[e[0]](*e[1:])
        if i == last + 1:
            part = GP[0]
            for k in range(1, NY):
                part += GP[k]
            GQ[mine] = part
            small(4, 36, GQ, mine, [(seq(y, z, oc), t), (seq(y, oz, c), t), (seq(y, oz, oc), t)])
    drain(GQ.at[pl.ds(0, 3)], small_recv.at[4])
    sums = GQ[0] + GQ[1] + GQ[2] + GQ[3]
    gain_f = gain[...].astype(jnp.float32)
    for i in range(8):
        head_out[i : i + 1, :] = gain_f[:, i * TOK : (i + 1) * TOK] * sums[i : i + 1, :]

    for copy in sends:
        copy.wait_send()
    drain(H.at[mine], hid_send.at[0])
    for i in range(2):
        drain(pair_block(i), hid_send.at[1 + i])


def scratch():
    f32, bf16 = jnp.float32, jnp.bfloat16
    V, S = pltpu.VMEM, pltpu.SemaphoreType.DMA
    out = [V((TOK, COLS), bf16)]
    out += [V((NY, 2, TOK, w), bf16) for w in WIDTHS]
    out += [V((4, ROWS, w), f32) for w in WIDTHS]
    out += [V((2, ROWS, w), f32) for w in WIDTHS]
    out += [V((ROWS, w), bf16) for w in WIDTHS] * 2
    out += [V((4, NY, 2, ROWS, TOK), bf16)]
    out += [V((n, 8, TOK), f32) for n in (8, 8, 8, 16)]
    out += [V((NY, 2 * TOK, TOK), f32)] * 2
    out += [V((NY, 8, TOK), f32), V((4, 8, TOK), f32)]
    out += [S((16 * C,)), S((16 * C,)), S((C,)), S((C,)), S((3 * C,)), S((3 * C,))]
    out += [S((39,)), S((5,)), S((11,)), S((11,)), S((2 + C,))]
    return out


def body(stream, hidden, final_gain, value_head, rewards, kl_terms, resets):
    vmem, hbm = pl.BlockSpec(memory_space=pltpu.VMEM), pl.BlockSpec(memory_space=pl.ANY)
    f32 = jnp.float32
    values, returns, grad_head, grad_down = pl.pallas_call(
        kernel,
        out_shape=(
            jax.ShapeDtypeStruct((1, TOK), f32),
            jax.ShapeDtypeStruct((1, TOK), f32),
            jax.ShapeDtypeStruct((8, TOK), f32),
            jax.ShapeDtypeStruct((ROWS, COLS), jnp.bfloat16),
        ),
        in_specs=[hbm, hbm] + [vmem] * 5,
        out_specs=(vmem,) * 4,
        scratch_shapes=scratch(),
        compiler_params=pltpu.CompilerParams(
            collective_id=0, has_side_effects=True, vmem_limit_bytes=60 * 1024 * 1024
        ),
    )(
        stream,
        hidden,
        final_gain.reshape(1, COLS),
        value_head.reshape(1, COLS),
        rewards.reshape(1, TOK),
        kl_terms.reshape(1, TOK),
        resets.reshape(1, TOK),
    )
    return (values.reshape(TOK), returns.reshape(TOK), grad_head.reshape(COLS), grad_down)


def solution(mesh):
    placed = (P("seq", "tp"), P("seq", None), P("tp"), P("tp"), P("seq"), P("seq"), P("seq"))
    return jax.shard_map(
        body,
        mesh=mesh,
        in_specs=placed,
        out_specs=(P("seq"), P("seq"), P("tp"), P("seq", "tp")),
        check_vma=False,
    )
```

time: 516 us -> 87.3 us (0.17)
  blocking collectives: 311 us -> 0 us
  loops' own time: 86.3 us -> 0 us
  Pallas kernels: 0 us -> 77.8 us
  local copies, waits for them, and re-layouts: 82.4 us -> 7.92 us
  between operations: 14.1 us -> 0.64 us
  matrix products: 11.6 us -> 0 us
  other arithmetic: 8.64 us -> 0 us
    psum x2 -> x0, blocking collectives: 171 us -> none  [the longest x1 145 us: body(): lax.psum(jnp.sum((value_error * inv_rms)[:, None] * stream_f, axis=0), 's...]
    unnamed x1 -> x0, blocking collectives: 140 us -> none
    another operation x1 -> x0, loops' own time: 86.3 us -> none  [prefix(): return lax.fori_loop(0, count - 1, step, total)]
    dynamic_slice x126 -> x0, local copies, waits for them, and re-layouts: 78.6 us -> none  [step(): longer = join(total, jax.tree.map(lambda part: part[position], pieces))]
    pallas_call x0 -> x1, Pallas kernels: none -> 77.8 us  [body(): pl.pallas_call(kernel, out_shape=(jax.ShapeDtypeStruct((1, TOK), f32), ja...]
    dot_general x1 -> x0, matrix products: 11.6 us -> none  [body(): jnp.dot(hidden, lax.all_gather(dstream, 'seq', axis=0, tiled=True), prefe...]
  transfers between devices with their start and end apart: 1 -> 0, of which waited for: 0 -> 0; matrix products, arithmetic and copies ran while one was open for 0% -> 0% of each run, Pallas kernels for 0% -> 0%
where the time goes in v1:
time: 87.3 us; the launch traced here: 86.3 us
  Pallas kernels  77.8 us (89%)
  local copies, waits for them, and re-layouts  7.92 us (9%)
    pallas_call x1, Pallas kernels, body(): pl.pallas_call(kernel, out_shape=(jax.ShapeDtypeStruct((1, TOK), f32), ja...  77.8 us
    unnamed x4, local copies, waits for them, and re-layouts  5.37 us

profile of v1, /device:TPU:1, one launch (start us, length us, event | category | flops | bytes accessed | tf_op | source)
XLA Modules:
  0.0 86.3 jit_solution(2156863422747114034)
XLA Ops:
  0.6 1.3 %reshape.32.refs_2_ = bf16[1,1024]{1,0:T(2,128)(2,1)} reshape(bf16[1024]{0:T(1024)(128)(2,1)} %param.9) | data formatting | bytes 4096 | tf_op jit(solution)/shard_map/reshape | solution.py:457
  1.9 1.3 %reshape.33.refs_3_ = bf16[1,1024]{1,0:T(2,128)(2,1)} reshape(bf16[1024]{0:T(1024)(128)(2,1)} %param.10) | data formatting | bytes 4096 | tf_op jit(solution)/shard_map/reshape | solution.py:458
  3.2 77.8 %shard_map.102 = (f32[1,128]{1,0:T(1,128)}, f32[1,128]{1,0:T(1,128)}, f32[8,128]{1,0:T(8,128)}, bf16[224,1024]{1,0:T(8,128)(2,1)}) custom-call(bf16[128,1024]{1,0:T(8,128)(2,1)} %refs_0_.1, bf16[224,8192]{1,0:T(8,128)(2,1)} %refs_1_.1, bf16[1,1024]{1,0:T(2,128)(2,1)} %reshape.32.refs_2_, bf16[1,1024]{1,0:T(2,128)(2,1)} %reshape.33.refs_3_, ...), custom_call_target="tpu_custom_call" | custom-call | tf_op jit(solution)/shard_map/pallas_call | solution.py:440
  81.0 1.1 %copy.15 = f32[128]{0:T(128)} copy(f32[128]{0:T(128)} %bitcast.11) | data formatting | bytes 1024
  82.1 1.1 %copy.16 = f32[128]{0:T(128)} copy(f32[128]{0:T(128)} %bitcast.10) | data formatting | bytes 1024
  83.3 1.3 %copy.17 = f32[1024]{0:T(1024)} copy(f32[1024]{0:T(1024)} %bitcast.6) | data formatting | bytes 8192
  84.5 1.8 %copy.18 = bf16[224,1024]{1,0:T(8,128)(2,1)} copy(bf16[224,1024]{1,0:T(8,128)(2,1)} %get-tuple-element.19) | data formatting | bytes 917504

commit v2 on v1

v2 whole, which is shorter than its diff:
```python
import functools

import jax
import jax.numpy as jnp
from jax import lax
from jax.experimental import pallas as pl
from jax.experimental.pallas import tpu as pltpu
from jax.sharding import PartitionSpec as P

MESH = pl.DeviceIdType.MESH
D = 8192
EPS = 1e-05
NY, NZ, NX, NT = 8, 4, 4, 8
TOK, COLS, ROWS = 128, 1024, 224
WIDTHS = (256, 256, 256, 256)
OFFS = tuple(sum(WIDTHS[:j]) for j in range(len(WIDTHS)))
C = len(WIDTHS)
LIMIT = {1: 1}
ROUND_FIRST = tuple(LIMIT)
FAR = {j: tuple(d for d in sorted(range(-3, 5), key=abs) if abs(d) > LIMIT[j]) for j in LIMIT}
HOPS = ((4, 3), (3, 4))
GROUPS = (("A", "B", "C"), ((-1, 0, 1, 2), (-2, 3, -3, 4)))
LAST_GROUPS = (("A", "B", "C"), ((0, 1), (-1, 2), (-2, 3), (-3, 4)))
QUARTERS = {"A": (0,), "B": (-1, 1), "C": (2,)}
START = 2.0
UNIT = tuple(w * 0.0055 for w in WIDTHS)
LAG = 2.0
FIRST, SECOND, COEF = 4.5, 11.5, 21.5
LOCAL, SHARE, PASS, LAST_HIDDEN = 15.0, (6.5, 9.0, 13.0, 17.0), (11.5, 14.2, 18.0, 22.0), 27.5
PAIR, AWAY = (0.0, 0.0, 4.2, 8.0), (2.6, 6.8, 10.5, 12.0)
SWAP, OVER = (10.5, 14.5, 18.0, 21.0), 17.0


def hops(direction, plane, j):
    return min(LIMIT[j], HOPS[direction][1]) if plane == 1 and j in LIMIT else HOPS[direction][plane]


ARRIVALS = {}
for _direction in (0, 1):
    for _plane in (0, 1):
        for _j in range(C):
            for _hop in range(hops(_direction, _plane, _j)):
                ARRIVALS[_direction, _plane, _j, _hop + 1] = len(ARRIVALS)


def ring_plan(direction):
    ready, order, arrival, now, due = {}, [], {}, 0.0, 0.0
    begin = []
    for j in range(C):
        begin.append(due - (4.0 if j == C - 1 else 0.0))
        due += UNIT[j] * sum(hops(direction, plane, j) for plane in (0, 1))
        ready[(0, j, 1)] = 0.0
        ready[(1, j, 1)] = SWAP[j]
    while ready:
        able = [m for m in ready if ready[m] <= now + 1e-9]
        if not able:
            now = min(ready.values())
            continue
        m = min(able, key=lambda m: (begin[m[1]] + 1.5 * (m[2] - 1), m[2], m[0]))
        del ready[m]
        plane, j, hop = m
        order.append((now, m))
        now += UNIT[j]
        arrival[m] = now + LAG
        if hop < hops(direction, plane, j):
            ready[(plane, j, hop + 1)] = arrival[m]
    return order, arrival


def timeline():
    todo, arrivals = [], []
    for direction in (0, 1):
        order, arrival = ring_plan(direction)
        arrivals.append(arrival)
        for t, (plane, j, hop) in order:
            if (plane, hop) != (0, 1) or t > START:
                todo.append((t, 0, 0.05, ("ring", direction, plane, j, hop)))
    todo += [(PAIR[k], 0, 0.05, ("pair", k)) for k in (2, 3)]
    todo += [(AWAY[j], 0, 0.05, ("away", j)) for j in range(C)]
    todo += [(SHARE[k], 0, 0.05, ("share", k)) for k in range(4)]
    todo += [(PASS[k], 0, 0.05, ("pass", k)) for k in range(4)]
    todo += [(LOCAL, 1, 0.5, ("local",)), (FIRST, 1, 0.2, ("first",)), (SECOND, 1, 0.4, ("second",))]
    todo += [(COEF + 0.1 * i, 2, 0.2, ("coef", i)) for i in range(NY)]
    hidden = {"A": SHARE[3] + 0.5, "B": PASS[3] + 0.3, "C": LAST_HIDDEN}
    groups = [LAST_GROUPS if j == C - 1 else GROUPS for j in range(C)]
    for j in range(C):
        times, over = ({}, {}), []
        for d in sorted(range(-3, 5), key=abs):
            own = 0.0 if d == 0 else arrivals[0 if d < 0 or d == 4 else 1][(0, j, abs(d))]
            times[0][d] = own
            if d in FAR.get(j, ()):
                own = max(own, OVER + 0.7 * len(over))
                over.append(d)
                todo.append((own, 0, 0.05, ("over", j, d)))
                times[1][d] = own + 5.0
            else:
                times[1][d] = SWAP[j] if d == 0 else arrivals[0 if d < 0 else 1][(1, j, abs(d))]
        for plane in (0, 1):
            for group in groups[j][plane]:
                if plane == 0:
                    n, t = 2 * len(QUARTERS[group]), max(hidden[group], *times[0].values())
                else:
                    n, t = len(group), max(hidden["C"], *(times[1][d] for d in group))
                todo.append((max(COEF + 1.5, t + 0.5), 3 + j, 0.05 + 0.135 * n, ("piece", j, plane, group)))
    now, order, left = 0.0, [], {j: len(groups[j][0]) + len(groups[j][1]) for j in range(C)}
    while todo:
        able = [e for e in todo if e[0] <= now + 1e-9]
        if not able:
            now = min(e[0] for e in todo)
            continue
        e = min(able, key=lambda e: (e[1], e[0]))
        todo.remove(e)
        order.append(e[3])
        now += e[2]
        if e[3][0] == "piece":
            j = e[3][1]
            left[j] -= 1
            if left[j] == 0:
                order.append(("reduce", j))
                if sum(left.values()):
                    todo.append((now + 4.0, 1, 0.2, ("swap", j)))
                else:
                    order += [e[3] for e in todo] + [("swap", j)]
                    todo = []
    return order + [("write", j) for j in range(C)]


def kernel(*refs):
    refs = list(refs)
    take = lambda n: [refs.pop(0) for _ in range(n)]
    stream, hidden, gain, head_in, rewards, kl_terms, resets = take(7)
    values_out, returns_out, head_out, down_out = take(4)
    (X,) = take(1)
    S, ACC, P1, T2, P2, O = take(C), take(C), take(C), take(C), take(C), take(C)
    H, ST, PA, PB, CO, AC, BC, GP, GQ, V, G, HV = take(12)
    ring_send, ring_recv, swap_send, swap_recv, down_send, down_recv, small_send, small_recv, hid_send, hid_recv, over_send, over_recv, local = take(13)

    s, t = lax.axis_index("seq"), lax.axis_index("tp")
    y, z, c = s // 8, (s // 2) % 4, s % 2
    zb, zp, q = z % 2, z // 2, s % 8
    h, x = t // 4, t % 4
    oz, oc = z + 1 - 2 * zb, 1 - c
    fz = z + 2 - 4 * zp
    mine = zb * 2 + c

    def seq(y, z, c):
        return (y * 4 + z) * 2 + c

    def up(d):
        return lax.rem(y + 16 + d, NY)

    def remote(src, dst, send, recv, device):
        return pltpu.make_async_remote_copy(
            src_ref=src, dst_ref=dst, send_sem=send, recv_sem=recv, device_id=device, device_id_type=MESH
        )

    def drain(ref, sem):
        pltpu.make_async_copy(ref, ref, sem).wait()

    line = []
    for d in range(1, 8):
        other = lax.rem(q + d, 8)
        line.append((y * 8 + other, t))
    column = [(seq(up(d), z, c), t) for d in range(1, NY)]
    far = [(seq(up(d), fz, c), t) for d in range(NY)]
    rank = [(s, lax.rem(t + d, NT)) for d in range(1, NT)]
    barrier = pltpu.get_barrier_semaphore()
    peers = line + column + far[1:] + rank
    for peer in peers:
        pl.semaphore_signal(barrier, inc=1, device_id=peer, device_id_type=MESH)

    x_copy = pltpu.make_async_copy(stream, X, local.at[0])
    x_copy.start()
    whole = pltpu.make_async_copy(hidden, HV, local.at[5 + 2 * C])
    whole.start()
    own_copies = []
    for j in range(C):
        own_copies.append(
            pltpu.make_async_copy(stream.at[:, pl.ds(OFFS[j], WIDTHS[j])], S[j].at[y, zp], local.at[1 + j])
        )
        own_copies[-1].start()

    def tokens(yy, zz, cc):
        return pl.ds(pl.multiple_of(seq(yy, zz, cc) * TOK, TOK), TOK)

    row_id = lax.broadcasted_iota(jnp.int32, (TOK, TOK), 0)
    col_id = lax.broadcasted_iota(jnp.int32, (TOK, TOK), 1)

    def to_col(row):
        return jnp.sum(jnp.where(row_id == col_id, row, 0.0), axis=1, keepdims=True)

    def to_row(col):
        return jnp.sum(jnp.where(row_id == col_id, col, 0.0), axis=0, keepdims=True)

    gain_f = gain[...].astype(jnp.float32)
    head = gain_f * head_in[...].astype(jnp.float32)
    head_rows = [head[n : n + 1, :] for n in range(COLS // TOK)]
    res_row = resets[...].astype(jnp.float32)
    before_col = jnp.sum(jnp.where(col_id < row_id, res_row, 0.0), axis=1, keepdims=True)
    before_row = jnp.sum(jnp.where(row_id < col_id, to_col(res_row), 0.0), axis=0, keepdims=True)
    total = jnp.sum(res_row, axis=1, keepdims=True)
    reward_col = to_col(rewards[...] - 0.2 * kl_terms[...])
    reach = (row_id >= col_id) & (before_col == before_row)
    local_row = jnp.sum(jnp.where(reach, reward_col, 0.0), axis=0, keepdims=True)
    pass_row = jnp.where(before_row == total, 1.0, 0.0)

    def put(ref, index, first, second):
        ref[index] = jnp.zeros((8, TOK), jnp.float32)
        ref[index, 0:1, :] = jnp.broadcast_to(first, (1, TOK))
        ref[index, 1:2, :] = jnp.broadcast_to(second, (1, TOK))

    put(PA, q, local_row[:, 0:1], pass_row[:, 0:1])
    x_copy.wait()
    squares, along = jnp.zeros((TOK, TOK), jnp.float32), jnp.zeros((TOK, TOK), jnp.float32)
    for n in range(COLS // TOK):
        xn = X[:, n * TOK : (n + 1) * TOK].astype(jnp.float32)
        squares += xn * xn
        along += xn * head_rows[n]
    put(
        ST,
        t,
        to_row(jnp.sum(squares, axis=1, keepdims=True)),
        to_row(jnp.sum(along, axis=1, keepdims=True)),
    )
    pl.semaphore_wait(barrier, len(peers))

    sends = []

    def go(copy):
        copy.start()
        sends.append(copy)

    def small(kind, ref, index, to):
        for peer in to:
            remote(ref.at[index], ref.at[index], small_send.at[kind], small_recv.at[kind], peer).start()

    def ring(direction, plane, j, hop):
        step = 1 if direction == 0 else -1
        slot = S[j].at[up(-step * (hop - 1)), zp if plane == 0 else 1 - zp]
        src = stream.at[:, pl.ds(OFFS[j], WIDTHS[j])] if (plane, hop) == (0, 1) else slot
        i = ARRIVALS[direction, plane, j, hop]
        return remote(src, slot, ring_send.at[direction * C + j], ring_recv.at[i], (seq(up(step), z, c), t))

    def swap(j):
        return remote(
            stream.at[:, pl.ds(OFFS[j], WIDTHS[j])], S[j].at[y, zp], swap_send.at[j], swap_recv.at[j], (seq(y, fz, c), t)
        )

    small(1, PA, q, line)
    small(0, ST, t, rank)
    first_sends = [{m[1]: at for at, m in ring_plan(d)[0] if m[0] == 0 and m[2] == 1} for d in (0, 1)]
    for j in range(C):
        for direction in (0, 1):
            if first_sends[direction][j] <= START:
                ring(direction, 0, j, 1).start()

    def pair_hidden(i, p, cc):
        yy = 2 * x + i
        return remote(
            HV.at[:, tokens(yy, 1 - zb + 2 * p, cc)], H.at[mine, yy, p],
            hid_send.at[1 + 2 * i + p], hid_recv.at[1 + 2 * i + p], (seq(y, oz, cc), t),
        )

    def do_pair(k):
        for cc in range(2):
            pair_hidden(k // 2, k % 2, cc).start()

    def do_away(j):
        swap(j).start()

    whole.wait()
    do_pair(0)
    do_pair(1)

    def core_hidden(yy, _):
        for p in range(2):
            remote(
                HV.at[:, tokens(yy, zb + 2 * p, oc)], H.at[mine, yy, p],
                hid_send.at[0], hid_recv.at[0], (seq(y, z, oc), t),
            ).start()
        return 0

    def own_hidden(yy, _):
        for p in range(2):
            pltpu.make_async_copy(HV.at[:, tokens(yy, zb + 2 * p, c)], H.at[mine, yy, p], local.at[1 + C]).start()
        return 0

    def do_local():
        lax.fori_loop(0, NY, core_hidden, 0)
        lax.fori_loop(0, NY, own_hidden, 0)

    def pair_block(k, owner):
        return H.at[pl.ds(2 * (1 - zb), 2), 2 * owner + k // 2, k % 2]

    def x_copy_to(direction, k, hop):
        step = 1 if direction == 0 else -1
        block = pair_block(k, lax.rem(x + 8 - step * (hop - 1), NX))
        n = 5 + (hop - 1) * 8 + direction * 4 + k
        return remote(block, block, hid_send.at[n], hid_recv.at[n], (s, h * 4 + lax.rem(x + 4 + step, NX)))

    seen = set()

    def arrived(direction, plane, j, hop):
        if (direction, plane, j, hop) not in seen:
            seen.add((direction, plane, j, hop))
            step = 1 if direction == 0 else -1
            i = ARRIVALS[direction, plane, j, hop]
            drain(S[j].at[up(-step * hop), zp if plane == 0 else 1 - zp], ring_recv.at[i])

    def own_in(j):
        if ("own", j) not in seen:
            seen.add(("own", j))
            own_copies[j].wait()

    def other_in(j):
        if ("swap", j) not in seen:
            seen.add(("swap", j))
            drain(S[j].at[y, 1 - zp], swap_recv.at[j])

    def do_ring(direction, plane, j, hop):
        if hop == 1 and plane == 1:
            other_in(j)
        elif hop > 1:
            arrived(direction, plane, j, hop - 1)
        ring(direction, plane, j, hop).start()

    def x_arrived(direction, k, hop):
        step = 1 if direction == 0 else -1
        owner = lax.rem(x + 8 - step * hop, NX)
        drain(pair_block(k, owner), hid_recv.at[5 + (hop - 1) * 8 + direction * 4 + k])

    def do_over(j, d):
        arrived(0 if d < 0 or d == 4 else 1, 0, j, abs(d))
        slot = S[j].at[up(d), zp]
        k = ROUND_FIRST.index(j)
        remote(slot, slot, over_send.at[k], over_recv.at[k * NY + d + 3], (seq(y, fz, c), t)).start()

    def over_in(j, d):
        drain(S[j].at[up(d), 1 - zp], over_recv.at[ROUND_FIRST.index(j) * NY + d + 3])

    def do_share(k):
        drain(pair_block(k, x), hid_recv.at[1 + k])
        for direction in (0, 1):
            go(x_copy_to(direction, k, 1))

    def do_pass(k):
        x_arrived(k % 2, k, 1)
        go(x_copy_to(k % 2, k, 2))

    def out_small(i):
        src = (V.at[0:1], V.at[1:2], G)[i]
        return pltpu.make_async_copy(src, (values_out, returns_out, head_out)[i], local.at[2 + 2 * C + i])

    def do_first():
        drain(PA.at[pl.ds(0, 7)], small_recv.at[1])
        value, keep = jnp.zeros((1, TOK), jnp.float32), jnp.ones((1, TOK), jnp.float32)
        for i in reversed(range(8)):
            value = PA[i, 0:1, :] + PA[i, 1:2, :] * value
            keep = PA[i, 1:2, :] * keep
        put(PB, y, value, keep)
        small(2, PB, y, column)

    def do_second():
        drain(PB.at[pl.ds(0, 7)], small_recv.at[2])
        carry = jnp.zeros((1, TOK), jnp.float32)
        my_y, my_q = jnp.full((1, TOK), y, jnp.int32), jnp.full((1, TOK), q, jnp.int32)
        for i in reversed(range(NY)):
            carry = jnp.where(my_y < i, PB[i, 0:1, :] + PB[i, 1:2, :] * carry, carry)
        for i in reversed(range(8)):
            carry = jnp.where(my_q < i, PA[i, 0:1, :] + PA[i, 1:2, :] * carry, carry)
        returns = local_row + pass_row * carry
        V[1:2, :] = returns
        out_small(1).start()
        drain(ST.at[pl.ds(0, 7)], small_recv.at[0])
        squares, along = jnp.zeros((1, TOK), jnp.float32), jnp.zeros((1, TOK), jnp.float32)
        for i in range(NT):
            squares += ST[i, 0:1, :]
            along += ST[i, 1:2, :]
        mean = squares * (1.0 / D) + EPS
        scale = lax.rsqrt(mean)
        scale = scale * (1.5 - 0.5 * mean * scale * scale)
        values = scale * along
        V[0:1, :] = values
        out_small(0).start()
        error = values - returns
        put(CO, y * 2 + zp, error * scale, error * (scale * scale * scale * along * (1.0 / D)))
        small(3, CO, y * 2 + zp, column + far)

    def do_coef(i):
        if i == 0:
            drain(CO.at[pl.ds(0, 15)], small_recv.at[3])
        for p in range(2):
            AC[i * 2 + p] = jnp.broadcast_to(to_col(CO[i * 2 + p, 0:1, :]), (TOK, TOK))
            BC[i * 2 + p] = jnp.broadcast_to(to_col(CO[i * 2 + p, 1:2, :]), (TOK, TOK))

    def hidden_in(part):
        if ("hidden", "A") not in seen:
            seen.add(("hidden", "A"))
            drain(H.at[mine], local.at[1 + C])
            drain(H.at[zb * 2 + oc], hid_recv.at[0])
        for name in "BC":
            if name <= part and ("hidden", name) not in seen:
                seen.add(("hidden", name))
                if name == "B":
                    for k in range(4):
                        x_arrived(1 - k % 2, k, 1)
                else:
                    for k in range(4):
                        x_arrived(k % 2, k, 2)

    def block_in(j, plane, d):
        side = 0 if d < 0 or (d == 4 and plane == 0) else 1
        if plane == 1 and d in FAR.get(j, ()):
            over_in(j, d)
        elif d == 0:
            (own_in, other_in)[plane](j)
        else:
            arrived(side, plane, j, abs(d))

    def do_piece(j, plane, group):
        w, off = WIDTHS[j], OFFS[j]
        p = zp if plane == 0 else 1 - zp
        if plane == 0:
            for d in range(-3, 5):
                block_in(j, 0, d)
            hidden_in(group)
            where = [2 * lax.rem(x + 4 + k, NX) + i for k in QUARTERS[group] for i in range(2)]
        else:
            for d in group:
                block_in(j, 1, d)
            hidden_in("C")
            where = [up(d) for d in group]
        grads, rows = [], [[] for _ in range(4)]
        for yy in where:
            a, b = AC[yy * 2 + p], BC[yy * 2 + p]
            xs = S[j][yy, p]
            parts = []
            for i in range(w // TOK):
                xi = xs[:, i * TOK : (i + 1) * TOK].astype(jnp.float32)
                n = off // TOK + i
                GP[yy * 2 + p, n : n + 1, :] = jnp.sum(a * xi, axis=0, keepdims=True)
                parts.append((a * head_rows[n] - b * xi).astype(jnp.bfloat16))
            grads.append(jnp.concatenate(parts, axis=1))
            for r in range(4):
                rows[r].append(H[r, yy, p])
        left = jnp.concatenate([jnp.concatenate(parts, axis=1) for parts in rows], axis=0)
        out = jnp.dot(left, jnp.concatenate(grads, axis=0), preferred_element_type=jnp.float32).reshape(4, ROWS, w)
        if ("sum", j) not in seen:
            seen.add(("sum", j))
            ACC[j][...] = out
        else:
            ACC[j][...] += out

    def core_copy(j, k):
        return remote(
            ACC[j].at[k * 2 + oc], P1[j].at[k], down_send.at[j * 3 + k], down_recv.at[j * 3 + k], (seq(y, z, oc), t)
        )

    def pair_copy(j):
        return remote(T2[j], P2[j], down_send.at[j * 3 + 2], down_recv.at[j * 3 + 2], (seq(y, oz, c), t))

    def do_reduce(j):
        go(core_copy(j, 1 - zb))
        go(core_copy(j, zb))

    def do_swap(j):
        core_copy(j, 1 - zb).wait_recv()
        T2[j][...] = (ACC[j][(1 - zb) * 2 + c] + P1[j][1 - zb]).astype(jnp.bfloat16)
        go(pair_copy(j))
        core_copy(j, zb).wait_recv()

    def out_copy(j):
        return pltpu.make_async_copy(O[j], down_out.at[:, pl.ds(OFFS[j], WIDTHS[j])], local.at[2 + C + j])

    def do_write(j):
        pair_copy(j).wait_recv()
        out = ACC[j][mine] + P1[j][zb] + P2[j][...].astype(jnp.float32)
        O[j][...] = out.astype(jnp.bfloat16)
        out_copy(j).start()

    events = {
        "ring": do_ring, "over": do_over, "share": do_share, "pass": do_pass, "first": do_first, "second": do_second,
        "coef": do_coef, "local": do_local, "pair": do_pair, "away": do_away, "piece": do_piece, "reduce": do_reduce, "swap": do_swap,
        "write": do_write,
    }
    order = timeline()
    last = max(i for i, e in enumerate(order) if e[0] == "piece")
    for i, e in enumerate(order):
        events[e[0]](*e[1:])
        if i == last + 1:
            part = GP[0]
            for k in range(1, 2 * NY):
                part += GP[k]
            GQ[mine] = part
            small(4, GQ, mine, [(seq(y, z, oc), t), (seq(y, oz, c), t), (seq(y, oz, oc), t)])
    drain(GQ.at[pl.ds(0, 3)], small_recv.at[4])
    sums = GQ[0] + GQ[1] + GQ[2] + GQ[3]
    G[...] = gain_f * sums
    out_small(2).start()

    for copy in sends:
        copy.wait_send()
    for kind, ref in enumerate((ST, PA, PB)):
        drain(ref.at[pl.ds(0, 7)], small_send.at[kind])
    drain(CO.at[pl.ds(0, 15)], small_send.at[3])
    drain(GQ.at[pl.ds(0, 3)], small_send.at[4])
    for direction in (0, 1):
        for j in range(C):
            n = sum(hops(direction, plane, j) for plane in (0, 1))
            drain(S[j].at[pl.ds(0, n), 0], ring_send.at[direction * C + j])
    for j in range(C):
        drain(S[j].at[0, 0], swap_send.at[j])
    for k, j in enumerate(ROUND_FIRST):
        drain(S[j].at[pl.ds(0, len(FAR[j])), 0], over_send.at[k])
    drain(H.at[mine], hid_send.at[0])
    for k in range(4):
        drain(pair_block(k, 0), hid_send.at[1 + k])
    for j in range(C):
        out_copy(j).wait()
    for i in range(3):
        out_small(i).wait()


def hand_over(*refs):
    for i in range(4):
        refs[4 + i][...] = refs[i][...]


def scratch():
    f32, bf16 = jnp.float32, jnp.bfloat16
    V, S = pltpu.VMEM, pltpu.SemaphoreType.DMA
    out = [V((TOK, COLS), bf16)]
    out += [V((NY, 2, TOK, w), bf16) for w in WIDTHS]
    out += [V((4, ROWS, w), f32) for w in WIDTHS]
    out += [V((2, ROWS, w), f32) for w in WIDTHS]
    out += [V((ROWS, w), bf16) for w in WIDTHS] * 3
    out += [V((4, NY, 2, ROWS, TOK), bf16)]
    out += [V((n, 8, TOK), f32) for n in (8, 8, 8, 16)]
    out += [V((NY * 2, TOK, TOK), f32)] * 2
    out += [V((NY * 2, 8, TOK), f32), V((4, 8, TOK), f32), V((8, TOK), f32), V((8, TOK), f32)]
    out += [V((ROWS, NY * NZ * 2 * TOK), bf16)]
    out += [S((2 * C,)), S((len(ARRIVALS),)), S((C,)), S((C,)), S((3 * C,)), S((3 * C,))]
    k = max(1, len(ROUND_FIRST))
    out += [S((5,)), S((5,)), S((21,)), S((21,)), S((k,)), S((NY * k,)), S((6 + 2 * C,))]
    return out


def body(stream, hidden, final_gain, value_head, rewards, kl_terms, resets):
    vmem, hbm = pl.BlockSpec(memory_space=pltpu.VMEM), pl.BlockSpec(memory_space=pl.ANY)
    f32 = jnp.float32
    shapes = (
        jax.ShapeDtypeStruct((1, TOK), f32),
        jax.ShapeDtypeStruct((1, TOK), f32),
        jax.ShapeDtypeStruct((8, TOK), f32),
        jax.ShapeDtypeStruct((ROWS, COLS), jnp.bfloat16),
    )
    parts = pl.pallas_call(
        kernel,
        out_shape=shapes,
        in_specs=[hbm, hbm] + [vmem] * 5,
        out_specs=(hbm,) * 4,
        scratch_shapes=scratch(),
        compiler_params=pltpu.CompilerParams(
            collective_id=0, has_side_effects=True, vmem_limit_bytes=60 * 1024 * 1024
        ),
    )(
        stream,
        hidden,
        final_gain.reshape(8, TOK),
        value_head.reshape(8, TOK),
        rewards.reshape(1, TOK),
        kl_terms.reshape(1, TOK),
        resets.reshape(1, TOK),
    )
    values, returns, grad_head, grad_down = pl.pallas_call(
        hand_over, out_shape=shapes, in_specs=[vmem] * 4, out_specs=(vmem,) * 4
    )(*parts)
    return (values.reshape(TOK), returns.reshape(TOK), grad_head.reshape(COLS), grad_down)


def solution(mesh):
    placed = (P("seq", "tp"), P("seq", None), P("tp"), P("tp"), P("seq"), P("seq"), P("seq"))
    return jax.shard_map(
        body,
        mesh=mesh,
        in_specs=placed,
        out_specs=(P("seq"), P("seq"), P("tp"), P("seq", "tp")),
        check_vma=False,
    )
```

time: 87.3 us -> 72 us (0.82)
  local copies, waits for them, and re-layouts: 7.92 us -> 0 us
  Pallas kernels: 77.8 us -> 71.2 us
    pallas_call x1 -> x2, Pallas kernels: 77.8 us -> 71.2 us  [the longest x1 69.4 us: body(): pl.pallas_call(kernel, out_shape=shapes, in_specs=[hbm, hbm] + [vmem] * 5...]
    unnamed x4 -> x0, local copies, waits for them, and re-layouts: 5.37 us -> none
    reshape x2 -> x0, local copies, waits for them, and re-layouts: 2.56 us -> none  [the longest x1 1.28 us: body(): final_gain.reshape(1, COLS)]
where the time goes in v2:
time: 72 us; the launch traced here: 71.9 us
  Pallas kernels  71.2 us (99%)
    pallas_call x1, Pallas kernels, body(): pl.pallas_call(kernel, out_shape=shapes, in_specs=[hbm, hbm] + [vmem] * 5...  69.4 us
    pallas_call x1, Pallas kernels, body(): pl.pallas_call(hand_over, out_shape=shapes, in_specs=[vmem] * 4, out_spec...  1.83 us

profile of v2, /device:TPU:1, one launch (start us, length us, event | category | flops | bytes accessed | tf_op | source)
XLA Modules:
  0.0 71.9 jit_solution(10798652926201848471)
XLA Ops:
  0.6 69.4 %shard_map.102 = (f32[1,128]{1,0:T(1,128)}, f32[1,128]{1,0:T(1,128)}, f32[8,128]{1,0:T(8,128)}, bf16[224,1024]{1,0:T(8,128)(2,1)}) custom-call(bf16[128,1024]{1,0:T(8,128)(2,1)} %refs_0_.1, bf16[224,8192]{1,0:T(8,128)(2,1)} %refs_1_.1, bf16[8,128]{1,0:T(8,128)(2,1)} %bitcast.8, bf16[8,128]{1,0:T(8,128)(2,1)} %bitcast.9, f32[1,128]{1,0:T(1,128)} %bitcast.10, ...), custom_call_target="tpu_custom_call" | custom-call | tf_op jit(solution)/shard_map/pallas_call | solution.py:557
  70.0 1.8 %shard_map.103 = (f32[1,128]{1,0:T(1,128)}, f32[1,128]{1,0:T(1,128)}, f32[8,128]{1,0:T(8,128)}, bf16[224,1024]{1,0:T(8,128)(2,1)}) custom-call(f32[1,128]{1,0:T(1,128)} %get-tuple-element.12.refs_0_, f32[1,128]{1,0:T(1,128)} %get-tuple-element.13.refs_1_, f32[8,128]{1,0:T(8,128)} %get-tuple-element.14.refs_2_, bf16[224,1024]{1,0:T(8,128)(2,1)} %get-tuple-element.15.refs_3_), custom_call_target="tpu_custom_call" | custom-call | tf_op jit(solution)/shard_map/pallas_call | solution.py:575
